TPU v7x, 256 devices: a whole 4x4x8 slice. The times are simulated.
256 devices in a mesh: dp: 64 (over y, z, core), rep: 4 (over x).
Axes of the slice: x: 4, y: 4, z: 8, core: 2. Of those that a mesh axis runs over, the one named last changes fastest.
Arguments:
- item_table: bfloat16 [32768, 512], P(('dp', 'rep')), may hold values from -6 to 6
- requests: int32 [256, 256, 2], P(('dp', 'rep')), may hold values from 0 to 127, as said below
- event_slot: int32 [131072], P(('dp', 'rep')), may hold values from 0 to 511, as said below
- lengths: int32 [256, 4], P(('dp', 'rep')), may hold values from 1 to 256, 512 in all within a row
- leaf_ids: int32 [131072, 8], P(('dp', 'rep')), may hold values from 0 to 31
- leaf_table: bfloat16 [256, 512], replicated, may hold values from -2.09375 to 2.09375
- w_in: bfloat16 [512, 2048], replicated, may hold values from -0.25 to 0.25
- w_out: bfloat16 [512, 512], replicated, may hold values from -0.25 to 0.25
- cotangent: bfloat16 [131072, 512], P(('dp', 'rep')), may hold values from -6 to 6
Outputs:
- output: bfloat16 [131072, 512], P(('dp', 'rep'))
- table_grad: float32 [32768, 512], P(('dp', 'rep'))
- leaf_grad: float32 [256, 512], replicated
- w_in_grad: float32 [512, 2048], replicated
- w_out_grad: float32 [512, 512], replicated
Inputs may be any that keep to these rules, and one draw needn't show every extreme that they name: `requests`: for each device and owner the 2 requested rows are distinct. `event_slot`: every one of a device's 512 slots is named by at least one of its events.
All inputs are finite; a program needn't handle non-finite values.
Results may differ from a plain program's by a relative error of at most 0.014.
Values may be sent and summed in bfloat16 or wider, within the bound.
A program may use at most 64 MiB of HBM per device.

v0:
```python
import jax
import jax.numpy as jnp
from jax import lax
from jax.sharding import PartitionSpec as P

HEADS = 4
epsilon = 1e-06


def normalize(values):
    center = values - jnp.mean(values, axis=-1, keepdims=True)
    spread = jnp.mean(center * center, axis=-1, keepdims=True)
    return center * lax.rsqrt(spread + epsilon)


def visible(lengths, count):
    ends = jnp.cumsum(lengths)
    places = jnp.arange(count, dtype=jnp.int32)
    segment = jnp.sum((places[:, None] >= ends[None, :]).astype(jnp.int32), axis=1)
    same = segment[:, None] == segment[None, :]
    return jnp.logical_and(same, places[None, :] <= places[:, None])


def front(rows, event_slot, lengths, leaf_ids, leaf_table, w_in):
    count = event_slot.shape[0]
    picker = (event_slot[:, None] == jnp.arange(rows.shape[0], dtype=jnp.int32)[None, :]).astype(
        jnp.bfloat16
    )
    leaves = leaf_table.shape[0] // leaf_ids.shape[1]
    onehot = (
        (leaf_ids[:, :, None] == jnp.arange(leaves, dtype=jnp.int32)[None, None, :])
        .reshape(count, -1)
        .astype(jnp.bfloat16)
    )
    inputs = (
        jnp.dot(picker, rows, preferred_element_type=jnp.float32)
        + jnp.dot(onehot, leaf_table, preferred_element_type=jnp.float32)
    ).astype(jnp.bfloat16)
    normed = normalize(inputs.astype(jnp.float32)).astype(jnp.bfloat16)
    hidden = jax.nn.silu(jnp.dot(normed, w_in, preferred_element_type=jnp.float32)).astype(
        jnp.bfloat16
    )
    width = w_in.shape[0]
    head_size = width // HEADS
    gates = hidden[:, 0:width]
    value_heads = hidden[:, width : 2 * width].reshape(count, HEADS, head_size)
    query_heads = hidden[:, 2 * width : 3 * width].reshape(count, HEADS, head_size)
    key_heads = hidden[:, 3 * width : 4 * width].reshape(count, HEADS, head_size)
    scores = jnp.einsum(
        "qhd,khd->hqk", query_heads, key_heads, preferred_element_type=jnp.float32
    ) * head_size ** (-0.5)
    allowed = visible(lengths, count)
    weights = jnp.where(allowed[None], jax.nn.silu(scores), 0.0).astype(jnp.bfloat16)
    mixed = jnp.einsum(
        "hqk,khd->qhd", weights, value_heads, preferred_element_type=jnp.float32
    ).reshape(count, width)
    gated = (normalize(mixed) * gates.astype(jnp.float32)).astype(jnp.bfloat16)
    return (inputs, gated)


def back(inputs, gated, w_out):
    return (
        jnp.dot(gated, w_out, preferred_element_type=jnp.float32) + inputs.astype(jnp.float32)
    ).astype(jnp.bfloat16)


def send_asked(wanted):
    result = lax.all_to_all(
        lax.all_to_all(wanted, "dp", split_axis=0, concat_axis=0, tiled=True),
        "rep",
        split_axis=1,
        concat_axis=1,
        tiled=True,
    )
    return result


def send_fetched(fetched):
    result = lax.all_to_all(
        lax.all_to_all(fetched, "dp", split_axis=0, concat_axis=0, tiled=True),
        "rep",
        split_axis=1,
        concat_axis=1,
        tiled=True,
    )
    return result


def send_returned(gradients):
    result = lax.all_to_all(
        lax.all_to_all(gradients, "dp", split_axis=0, concat_axis=0, tiled=True),
        "rep",
        split_axis=1,
        concat_axis=1,
        tiled=True,
    )
    return result


def on_device(
    item_table, requests, event_slot, lengths, leaf_ids, leaf_table, w_in, w_out, cotangent
):
    data_count = lax.axis_size("dp")
    replica_count = lax.axis_size("rep")
    width = item_table.shape[1]
    wanted = requests.reshape(data_count, replica_count, -1)
    asked = send_asked(wanted)
    fetched = item_table[asked]
    arrived = send_fetched(fetched).reshape(-1, width)

    def local_front(rows, table_leaf, weight_in):
        return front(rows, event_slot, lengths[0], leaf_ids, table_leaf, weight_in)

    (inputs, gated), pull_front = jax.vjp(local_front, arrived, leaf_table, w_in)
    output, pull_back = jax.vjp(back, inputs, gated, w_out)
    d_inputs, d_gated, d_out = pull_back(cotangent)
    d_rows, d_leaf, d_in = pull_front((d_inputs, d_gated))
    returned = send_returned(d_rows.reshape(data_count, replica_count, -1, width))
    leaf_sum, in_sum, out_sum = lax.psum(
        (d_leaf.astype(jnp.float32), d_in.astype(jnp.float32), d_out.astype(jnp.float32)),
        ("dp", "rep"),
    )
    table_grad = (
        jnp.zeros(item_table.shape, jnp.float32)
        .at[asked.reshape(-1)]
        .add(returned.reshape(-1, width).astype(jnp.float32))
    )
    share = 1.0 / (data_count * replica_count)
    return (output, table_grad, leaf_sum * share, in_sum * share, out_sum * share)


def solution(mesh):
    return jax.shard_map(
        on_device,
        mesh=mesh,
        in_specs=(
            P(("dp", "rep"), None),
            P(("dp", "rep"), None, None),
            P(("dp", "rep")),
            P(("dp", "rep"), None),
            P(("dp", "rep"), None),
            P(),
            P(),
            P(),
            P(("dp", "rep"), None),
        ),
        out_specs=(P(("dp", "rep"), None), P(("dp", "rep"), None), P(), P(), P()),
        check_vma=False,
    )
```

profile of v0, /device:TPU:97, one launch (start us, length us, event | category | flops | bytes accessed | tf_op | source)
XLA Modules:
  0.0 433.1 jit_solution(8049075674224172676)
XLA Ops:
  8.2 18.3 %all_to_all.30 = s32[64,4,2]{1,2,0:T(2,128)S(1)} all-to-all(s32[64,4,2]{1,2,0:T(2,128)S(1)} %copy.143), channel_id=1, replica_groups=mesh['dp'=64,'rep'=4] {'dp'}, dimensions={0} | all-to-all | bytes 4096 | tf_op jit(solution)/shard_map/all_to_all | solution.py:69
  26.7 7.9 %all_to_all.31 = s32[4,1,128]{2,1,0:T(1,128)S(1)} all-to-all(s32[4,1,128]{2,1,0:T(1,128)S(1)} %reshape.234), channel_id=1, replica_groups=mesh['dp'=64,'rep'=4] {'rep'}, dimensions={0} | all-to-all | bytes 4096 | tf_op jit(solution)/shard_map/all_to_all | solution.py:68
  36.2 2.9 gather_fusion
  40.1 8.5 %all-to-all-start.2 = ((bf16[64,4,2,512]{3,2,1,0:T(2,128)(2,1)}), bf16[64,4,2,512]{3,2,1,0:T(2,128)(2,1)S(1)}, u32[]{:S(2)}, u32[]{:S(2)}) async-start(bf16[64,4,2,512]{3,2,1,0:T(2,128)(2,1)} %reshape.215), calls=%async_computation.2 | async-start | bytes 1048576 | tf_op jit(solution)/shard_map/all_to_all | solution.py:80
  50.1 15.3 %all-to-all-done.2 = bf16[64,4,2,512]{3,2,1,0:T(2,128)(2,1)S(1)} async-done(((bf16[64,4,2,512]{3,2,1,0:T(2,128)(2,1)}), bf16[64,4,2,512]{3,2,1,0:T(2,128)(2,1)S(1)}, u32[]{:S(2)}, u32[]{:S(2)}) %all-to-all-start.2) | async-done | bytes 524320 | tf_op jit(solution)/shard_map/all_to_all | solution.py:80
  66.6 3.5 all-to-all-start.3
  70.5 2.3 fusion.42
  72.8 7.3 %all-to-all-done.3 = bf16[64,4,2,512]{3,2,0,1:T(2,128)(2,1)S(1)} async-done(((bf16[64,4,2,512]{3,2,0,1:T(2,128)(2,1)}), bf16[64,4,2,512]{3,2,0,1:T(2,128)(2,1)S(1)}, u32[]{:S(2)}, u32[]{:S(2)}) %all-to-all-start.3) | async-done | bytes 524320 | tf_op jit(solution)/shard_map/all_to_all | solution.py:79
  86.0 3.9 multiply_convert_fusion
  96.5 4.8 %select_convert_fusion = (bf16[4,512,512]{2,1,0:T(8,128)(2,1)S(1)}, f32[4,512,512]{2,1,0:T(8,128)}) fusion(pred[512,512]{1,0:T(8,128)(4,1)S(1)} %fusion.22, bf16[512,4,128]{0,2,1:T(8,128)(2,1)} %bitcast.68, bf16[512,4,128]{0,2,1:T(8,128)(2,1)} %bitcast.70), kind=kOutput, calls=%fused_computation.11 | convolution fusion | flops 275775488 | bytes 7602176 | tf_op jit(solution)/shard_map/jvp(qhd,khd->hqk)/dot_general | solution.py:49
  103.9 2.6 copy.171
  109.3 3.0 fusion.40
  115.3 5.1 %fusion.4 = bf16[4,512,512]{2,1,0:T(8,128)(2,1)S(1)} fusion(f32[4,512,512]{2,1,0:T(8,128)} %get-tuple-element.57, pred[512,512]{1,0:T(8,128)(4,1)S(1)} %fusion.22, bf16[4,128,512]{2,1,0:T(8,128)(2,1)} %bitcast.72, bf16[64,4,8,128]{3,2,1,0:T(8,128)(2,1)} %get-tuple-element.46), kind=kOutput, calls=%fused_computation.10 | convolution fusion | flops 283115520 | bytes 7602176 | tf_op jit(solution)/shard_map/transpose(jvp(hqk,khd->qhd))/dot_general | solution.py:54
  130.9 3.6 fusion
  134.5 3.3 fusion.5
  143.3 2.5 convolution_convert_fusion.1
  147.9 6.8 %all-to-all-start.4 = ((bf16[64,4,2,512]{3,2,1,0:T(2,128)(2,1)}), bf16[64,4,2,512]{3,2,1,0:T(2,128)(2,1)}, u32[]{:S(2)}, u32[]{:S(2)}) async-start(bf16[64,4,2,512]{3,2,1,0:T(2,128)(2,1)} %reshape.212), calls=%async_computation.4 | async-start | bytes 1048576 | tf_op jit(solution)/shard_map/all_to_all | solution.py:91
  155.0 17.6 %all-to-all-done.4 = bf16[64,4,2,512]{3,2,1,0:T(2,128)(2,1)} async-done(((bf16[64,4,2,512]{3,2,1,0:T(2,128)(2,1)}), bf16[64,4,2,512]{3,2,1,0:T(2,128)(2,1)}, u32[]{:S(2)}, u32[]{:S(2)}) %all-to-all-start.4) | async-done | bytes 524320 | tf_op jit(solution)/shard_map/all_to_all | solution.py:91
  174.8 4.4 %all-to-all-start.5 = ((bf16[64,4,2,512]{3,2,0,1:T(2,128)(2,1)}), bf16[64,4,2,512]{3,2,0,1:T(2,128)(2,1)}, u32[]{:S(2)}, u32[]{:S(2)}) async-start(bf16[64,4,2,512]{3,2,0,1:T(2,128)(2,1)} %copy.164), calls=%async_computation.5 | async-start | bytes 1048576 | tf_op jit(solution)/shard_map/all_to_all | solution.py:90
  179.2 2.3 fusion.11
  183.6 5.3 %all-to-all-done.5 = bf16[64,4,2,512]{3,2,0,1:T(2,128)(2,1)} async-done(((bf16[64,4,2,512]{3,2,0,1:T(2,128)(2,1)}), bf16[64,4,2,512]{3,2,0,1:T(2,128)(2,1)}, u32[]{:S(2)}, u32[]{:S(2)}) %all-to-all-start.5) | async-done | bytes 524320 | tf_op jit(solution)/shard_map/all_to_all | solution.py:90
  192.6 4.9 %scatter_custom_fusion = f32[128,512]{1,0:T(8,128)} fusion(s32[512]{0:T(512)S(1)} %bitcast.79, f32[512,512]{1,0:T(8,128)} %reshape.226, f32[]{:T(128)} %constant.15.clone.1), kind=kCustom, calls=%fused_computation.74 | custom fusion | flops 262144 | bytes 262656 | tf_op jit(solution)/shard_map/scatter-add | solution.py:126
  197.6 221.8 %all-reduce.7.cloned.1.call-done = (f32[256,512]{1,0:T(8,128)}, f32[512,2048]{1,0:T(8,128)}, f32[512,512]{1,0:T(8,128)}) async-done(((f32[256,512]{1,0:T(8,128)}, f32[512,2048]{1,0:T(8,128)}, f32[512,512]{1,0:T(8,128)}), (f32[256,512]{1,0:T(8,128)}, f32[512,2048]{1,0:T(8,128)}, f32[512,512]{1,0:T(8,128)})) %all-reduce.7.cloned.1.call-update) | async-done | bytes 5767184 | tf_op jit(solution)/shard_map/psum | solution.py:119
  419.4 4.9 %broadcast_multiply_fusion = f32[512,2048]{1,0:T(8,128)} fusion(f32[512,2048]{1,0:T(8,128)} %get-tuple-element.41), kind=kLoop, calls=%fused_computation.17 | loop fusion | flops 1048576 | bytes 8388608 | tf_op jit(solution)/shard_map/mul | solution.py:129
  (107 shorter events, 55.9 us)
Async XLA Ops:
  7.2 78.8 %copy-start = (bf16[512,2048]{1,0:T(8,128)(2,1)S(1)}, bf16[512,2048]{1,0:T(8,128)(2,1)}, u32[]{:S(2)}) copy-start(bf16[512,2048]{1,0:T(8,128)(2,1)} %param.15) | copy-start | bytes 6291460
  7.2 41.5 %copy-start.21 = (s32[1,4]{1,0:T(1,128)S(1)}, s32[1,4]{1,0:T(1,128)}, u32[]{:S(2)}) copy-start(s32[1,4]{1,0:T(1,128)} %param.12) | copy-start | bytes 52
  7.2 41.7 %copy-start.4 = (bf16[512,512]{1,0:T(8,128)(2,1)S(1)}, bf16[512,512]{1,0:T(8,128)(2,1)}, u32[]{:S(2)}) copy-start(bf16[512,512]{1,0:T(8,128)(2,1)} %param.17) | copy-start | bytes 1572868
  26.5 23.4 %copy-start.18 = (s32[512,8]{0,1:T(8,128)S(1)}, s32[512,8]{0,1:T(8,128)}, u32[]{:S(2)}) copy-start(s32[512,8]{0,1:T(8,128)} %param.13) | copy-start | bytes 49156
  40.1 43.1 %copy-start.19 = (s32[512]{0:T(512)S(1)}, s32[512]{0:T(512)}, u32[]{:S(2)}) copy-start(s32[512]{0:T(512)} %param.11) | copy-start | bytes 6148
  40.1 25.3 %all-to-all-start.2 = ((bf16[64,4,2,512]{3,2,1,0:T(2,128)(2,1)}), bf16[64,4,2,512]{3,2,1,0:T(2,128)(2,1)S(1)}, u32[]{:S(2)}, u32[]{:S(2)}) async-start(bf16[64,4,2,512]{3,2,1,0:T(2,128)(2,1)} %reshape.215), calls=%async_computation.2 | async-start | bytes 1048576 | tf_op jit(solution)/shard_map/all_to_all | solution.py:80
  66.6 13.5 %all-to-all-start.3 = ((bf16[64,4,2,512]{3,2,0,1:T(2,128)(2,1)}), bf16[64,4,2,512]{3,2,0,1:T(2,128)(2,1)S(1)}, u32[]{:S(2)}, u32[]{:S(2)}) async-start(bf16[64,4,2,512]{3,2,0,1:T(2,128)(2,1)} %copy.146), calls=%async_computation.3 | async-start | bytes 1048576 | tf_op jit(solution)/shard_map/all_to_all | solution.py:79
  70.0 349.4 %all-reduce.7.cloned.1.call-start = ((), (), s32[]{:S(2)}) async-start(), calls=%async_computation.6 | async-start | bytes 11534336 | tf_op jit(solution)/shard_map/psum | solution.py:119
  89.9 1.4 copy-start.7
  96.5 4.9 %copy-start.8 = (bf16[64,4,8,128]{3,2,1,0:T(8,128)(2,1)S(1)}, bf16[64,4,8,128]{3,2,1,0:T(8,128)(2,1)}, u32[]{:S(2)}) copy-start(bf16[64,4,8,128]{3,2,1,0:T(8,128)(2,1)} %get-tuple-element.46) | copy-start | bytes 1572868
  101.3 2.6 copy-start.2
  115.3 5.1 %copy-start.10 = (bf16[512,512]{0,1:T(8,128)(2,1)S(1)}, bf16[512,512]{0,1:T(8,128)(2,1)}, u32[]{:S(2)}) copy-start(bf16[512,512]{0,1:T(8,128)(2,1)} %copy.176) | copy-start | bytes 1572868
  115.3 6.3 %copy-start.11 = (bf16[512,512]{0,1:T(8,128)(2,1)S(1)}, bf16[512,512]{0,1:T(8,128)(2,1)}, u32[]{:S(2)}) copy-start(bf16[512,512]{0,1:T(8,128)(2,1)} %copy.177) | copy-start | bytes 1572868
  120.4 2.9 copy-start.3
  120.4 2.9 copy-start.13
  137.8 1.3 copy-start.17
  137.8 1.6 copy-start.9
  137.8 4.0 copy-start.5
  141.8 1.5 copy-start.20
  143.3 35.9 %copy-start.6 = (bf16[512,512]{1,0:T(8,128)(2,1)S(1)}, bf16[512,512]{1,0:T(8,128)(2,1)}, u32[]{:S(2)}) copy-start(bf16[512,512]{1,0:T(8,128)(2,1)} %get-tuple-element.45) | copy-start | bytes 1572868
  147.9 24.7 %all-to-all-start.4 = ((bf16[64,4,2,512]{3,2,1,0:T(2,128)(2,1)}), bf16[64,4,2,512]{3,2,1,0:T(2,128)(2,1)}, u32[]{:S(2)}, u32[]{:S(2)}) async-start(bf16[64,4,2,512]{3,2,1,0:T(2,128)(2,1)} %reshape.212), calls=%async_computation.4 | async-start | bytes 1048576 | tf_op jit(solution)/shard_map/all_to_all | solution.py:91
  174.8 14.1 %all-to-all-start.5 = ((bf16[64,4,2,512]{3,2,0,1:T(2,128)(2,1)}), bf16[64,4,2,512]{3,2,0,1:T(2,128)(2,1)}, u32[]{:S(2)}, u32[]{:S(2)}) async-start(bf16[64,4,2,512]{3,2,0,1:T(2,128)(2,1)} %copy.164), calls=%async_computation.5 | async-start | bytes 1048576 | tf_op jit(solution)/shard_map/all_to_all | solution.py:90
  419.4 4.9 %copy-start.14 = (f32[512,512]{1,0:T(8,128)S(1)}, f32[512,512]{1,0:T(8,128)}, u32[]{:S(2)}) copy-start(f32[512,512]{1,0:T(8,128)} %get-tuple-element.42) | copy-start | bytes 3145732
  419.4 6.0 %copy-start.15 = (f32[256,512]{1,0:T(8,128)S(1)}, f32[256,512]{1,0:T(8,128)}, u32[]{:S(2)}) copy-start(f32[256,512]{1,0:T(8,128)} %get-tuple-element.40) | copy-start | bytes 1572868
  (3 other events, 2.3 us)
Sparse Core Ops, SparseCore 0:
  143.4 275.9 all-reduce.6
where the time goes:
time: 434 us; the launch traced here: 433 us
  waiting for transfers between devices  267 us (62%)
  local copies, waits for them, and re-layouts  40.3 us (9%)
  matrix products  37.4 us (9%)
  blocking collectives  26.2 us (6%)
  other arithmetic  24 us (6%)
  starting transfers between devices  23.4 us (5%)
  between operations  14.4 us (3%)
    psum x1, waiting for transfers between devices, on_device(): lax.psum((d_leaf.astype(jnp.float32), d_in.astype(jnp.float32), d_out.ast...  222 us
    all_to_all x1, blocking collectives, send_asked(): lax.all_to_all(wanted, 'dp', split_axis=0, concat_axis=0, tiled=True)  18.3 us
    all_to_all x1, waiting for transfers between devices, send_returned(): lax.all_to_all(gradients, 'dp', split_axis=0, concat_axis=0, tiled=True)  17.6 us
    all_to_all x1, waiting for transfers between devices, send_fetched(): lax.all_to_all(fetched, 'dp', split_axis=0, concat_axis=0, tiled=True)  15.3 us
  transfers between devices with their start and end apart: 5, of which 5 were waited for; matrix products, arithmetic and copies ran while one was open for 6% of the time, Pallas kernels for 0%

commit v1 on v0

--- a/solution.py
+++ b/solution.py
@@ -117,8 +117,11 @@
     d_rows, d_leaf, d_in = pull_front((d_inputs, d_gated))
     returned = send_returned(d_rows.reshape(data_count, replica_count, -1, width))
     leaf_sum, in_sum, out_sum = lax.psum(
-        (d_leaf.astype(jnp.float32), d_in.astype(jnp.float32), d_out.astype(jnp.float32)),
-        ("dp", "rep"),
+        lax.psum(
+            (d_leaf.astype(jnp.float32), d_in.astype(jnp.float32), d_out.astype(jnp.float32)),
+            axis_name="dp",
+        ),
+        axis_name="rep",
     )
     table_grad = (
         jnp.zeros(item_table.shape, jnp.float32)

time: 434 us -> 488 us (1.12)
  waiting for transfers between devices: 267 us -> 316 us
    psum x0 -> x1, waiting for transfers between devices: none -> 70 us  [on_device(): lax.psum(lax.psum((d_leaf.astype(jnp.float32), d_in.astype(jnp.float32),...]
    psum x1, waiting for transfers between devices: 222 us -> 196 us  [on_device(): lax.psum((d_leaf.astype(jnp.float32), d_in.astype(jnp.float32), d_out.ast...]
    all_to_all x1, waiting for transfers between devices: 5.33 us -> 11.2 us  [send_returned(): lax.all_to_all(lax.all_to_all(gradients, 'dp', split_axis=0, concat_axis=...]
  transfers between devices with their start and end apart: 5 -> 6, of which waited for: 5 -> 6; matrix products, arithmetic and copies ran while one was open for 6% -> 5% of each run, Pallas kernels for 0% -> 0%
where the time goes in v1:
time: 488 us; the launch traced here: 485 us
  waiting for transfers between devices  316 us (65%)
  local copies, waits for them, and re-layouts  43.3 us (9%)
  matrix products  37.4 us (8%)
  blocking collectives  26.2 us (5%)
  starting transfers between devices  24 us (5%)
  other arithmetic  23.4 us (5%)
  between operations  14.4 us (3%)
    psum x1, waiting for transfers between devices, on_device(): lax.psum((d_leaf.astype(jnp.float32), d_in.astype(jnp.float32), d_out.ast...  196 us
    psum x1, waiting for transfers between devices, on_device(): lax.psum(lax.psum((d_leaf.astype(jnp.float32), d_in.astype(jnp.float32),...  70 us
    all_to_all x1, blocking collectives, send_asked(): lax.all_to_all(wanted, 'dp', split_axis=0, concat_axis=0, tiled=True)  18.3 us
    all_to_all x1, waiting for transfers between devices, send_returned(): lax.all_to_all(gradients, 'dp', split_axis=0, concat_axis=0, tiled=True)  16.3 us
    all_to_all x1, waiting for transfers between devices, send_fetched(): lax.all_to_all(fetched, 'dp', split_axis=0, concat_axis=0, tiled=True)  15.3 us
    all_to_all x1, waiting for transfers between devices, send_returned(): lax.all_to_all(lax.all_to_all(gradients, 'dp', split_axis=0, concat_axis=...  11.2 us
  transfers between devices with their start and end apart: 6, of which 6 were waited for; matrix products, arithmetic and copies ran while one was open for 5% of the time, Pallas kernels for 0%

profile of v1, /device:TPU:97, one launch (start us, length us, event | category | flops | bytes accessed | tf_op | source)
XLA Modules:
  0.0 484.9 jit_solution(11517831942194785652)
XLA Ops:
  8.2 18.3 %all_to_all.30 = s32[64,4,2]{1,2,0:T(2,128)S(1)} all-to-all(s32[64,4,2]{1,2,0:T(2,128)S(1)} %copy.143), channel_id=1, replica_groups=mesh['dp'=64,'rep'=4] {'dp'}, dimensions={0} | all-to-all | bytes 4096 | tf_op jit(solution)/shard_map/all_to_all | solution.py:69
  26.7 7.9 %all_to_all.31 = s32[4,1,128]{2,1,0:T(1,128)S(1)} all-to-all(s32[4,1,128]{2,1,0:T(1,128)S(1)} %reshape.234), channel_id=1, replica_groups=mesh['dp'=64,'rep'=4] {'rep'}, dimensions={0} | all-to-all | bytes 4096 | tf_op jit(solution)/shard_map/all_to_all | solution.py:68
  36.2 3.6 gather_fusion
  41.8 8.5 %all-to-all-start.2 = ((bf16[64,4,2,512]{3,2,1,0:T(2,128)(2,1)}), bf16[64,4,2,512]{3,2,1,0:T(2,128)(2,1)S(1)}, u32[]{:S(2)}, u32[]{:S(2)}) async-start(bf16[64,4,2,512]{3,2,1,0:T(2,128)(2,1)} %reshape.215), calls=%async_computation.2 | async-start | bytes 1048576 | tf_op jit(solution)/shard_map/all_to_all | solution.py:80
  51.8 15.3 %all-to-all-done.2 = bf16[64,4,2,512]{3,2,1,0:T(2,128)(2,1)S(1)} async-done(((bf16[64,4,2,512]{3,2,1,0:T(2,128)(2,1)}), bf16[64,4,2,512]{3,2,1,0:T(2,128)(2,1)S(1)}, u32[]{:S(2)}, u32[]{:S(2)}) %all-to-all-start.2) | async-done | bytes 524320 | tf_op jit(solution)/shard_map/all_to_all | solution.py:80
  68.3 3.5 all-to-all-start.3
  74.5 7.3 %all-to-all-done.3 = bf16[64,4,2,512]{3,2,0,1:T(2,128)(2,1)S(1)} async-done(((bf16[64,4,2,512]{3,2,0,1:T(2,128)(2,1)}), bf16[64,4,2,512]{3,2,0,1:T(2,128)(2,1)S(1)}, u32[]{:S(2)}, u32[]{:S(2)}) %all-to-all-start.3) | async-done | bytes 524320 | tf_op jit(solution)/shard_map/all_to_all | solution.py:79
  87.8 3.8 multiply_convert_fusion
  98.3 4.9 %select_convert_fusion = (bf16[4,512,512]{2,1,0:T(8,128)(2,1)S(1)}, f32[4,512,512]{2,1,0:T(8,128)}) fusion(pred[512,512]{1,0:T(8,128)(4,1)S(1)} %fusion.22, bf16[512,4,128]{0,2,1:T(8,128)(2,1)} %bitcast.68, bf16[512,4,128]{0,2,1:T(8,128)(2,1)} %bitcast.70), kind=kOutput, calls=%fused_computation.11 | convolution fusion | flops 275775488 | bytes 7602176 | tf_op jit(solution)/shard_map/jvp(qhd,khd->hqk)/dot_general | solution.py:49
  105.7 2.6 copy.171
  111.1 3.0 fusion.40
  117.1 5.1 %fusion.4 = bf16[4,512,512]{2,1,0:T(8,128)(2,1)S(1)} fusion(f32[4,512,512]{2,1,0:T(8,128)} %get-tuple-element.60, pred[512,512]{1,0:T(8,128)(4,1)S(1)} %fusion.22, bf16[4,128,512]{2,1,0:T(8,128)(2,1)} %bitcast.72, bf16[64,4,8,128]{3,2,1,0:T(8,128)(2,1)} %get-tuple-element.49), kind=kOutput, calls=%fused_computation.10 | convolution fusion | flops 283115520 | bytes 7602176 | tf_op jit(solution)/shard_map/transpose(jvp(hqk,khd->qhd))/dot_general | solution.py:54
  132.7 3.6 fusion
  136.3 3.3 fusion.5
  145.1 196.2 %all-reduce.9.cloned.1.call-done = (f32[256,512]{1,0:T(8,128)}, f32[512,2048]{1,0:T(8,128)}, f32[512,512]{1,0:T(8,128)}) async-done(((f32[256,512]{1,0:T(8,128)}, f32[512,2048]{1,0:T(8,128)}, f32[512,512]{1,0:T(8,128)}), (f32[256,512]{1,0:T(8,128)}, f32[512,2048]{1,0:T(8,128)}, f32[512,512]{1,0:T(8,128)})) %all-reduce.9.cloned.1.call-update) | async-done | bytes 5767184 | tf_op jit(solution)/shard_map/psum | solution.py:120
  341.3 2.5 convolution_convert_fusion.1
  345.9 7.3 %all-to-all-start.4 = ((bf16[64,4,2,512]{3,2,1,0:T(2,128)(2,1)}), bf16[64,4,2,512]{3,2,1,0:T(2,128)(2,1)}, u32[]{:S(2)}, u32[]{:S(2)}) async-start(bf16[64,4,2,512]{3,2,1,0:T(2,128)(2,1)} %reshape.212), calls=%async_computation.4 | async-start | bytes 1048576 | tf_op jit(solution)/shard_map/all_to_all | solution.py:91
  353.5 16.3 %all-to-all-done.4 = bf16[64,4,2,512]{3,2,1,0:T(2,128)(2,1)} async-done(((bf16[64,4,2,512]{3,2,1,0:T(2,128)(2,1)}), bf16[64,4,2,512]{3,2,1,0:T(2,128)(2,1)}, u32[]{:S(2)}, u32[]{:S(2)}) %all-to-all-start.4) | async-done | bytes 524320 | tf_op jit(solution)/shard_map/all_to_all | solution.py:91
  372.1 4.4 all-to-all-start.5
  376.5 2.3 fusion.11
  380.9 11.2 %all-to-all-done.5 = bf16[64,4,2,512]{3,2,0,1:T(2,128)(2,1)} async-done(((bf16[64,4,2,512]{3,2,0,1:T(2,128)(2,1)}), bf16[64,4,2,512]{3,2,0,1:T(2,128)(2,1)}, u32[]{:S(2)}, u32[]{:S(2)}) %all-to-all-start.5) | async-done | bytes 524320 | tf_op jit(solution)/shard_map/all_to_all | solution.py:90
  397.0 4.2 scatter_custom_fusion
  401.3 70.0 %all-reduce.11.cloned.1.call-done = (f32[256,512]{1,0:T(8,128)}, f32[512,2048]{1,0:T(8,128)}, f32[512,512]{1,0:T(8,128)}) async-done(((f32[256,512]{1,0:T(8,128)}, f32[512,2048]{1,0:T(8,128)}, f32[512,512]{1,0:T(8,128)}), (f32[256,512]{1,0:T(8,128)}, f32[512,2048]{1,0:T(8,128)}, f32[512,512]{1,0:T(8,128)})) %all-reduce.11.cloned.1.call-update) | async-done | bytes 5767184 | tf_op jit(solution)/shard_map/psum | solution.py:119
  471.3 4.9 %broadcast_multiply_fusion = f32[512,2048]{1,0:T(8,128)} fusion(f32[512,2048]{1,0:T(8,128)} %get-tuple-element.44), kind=kLoop, calls=%fused_computation.17 | loop fusion | flops 1048576 | bytes 8388608 | tf_op jit(solution)/shard_map/mul | solution.py:132
  (110 shorter events, 60.5 us)
Async XLA Ops:
  7.2 80.6 %copy-start = (bf16[512,2048]{1,0:T(8,128)(2,1)S(1)}, bf16[512,2048]{1,0:T(8,128)(2,1)}, u32[]{:S(2)}) copy-start(bf16[512,2048]{1,0:T(8,128)(2,1)} %param.15) | copy-start | bytes 6291460
  7.2 43.2 %copy-start.21 = (s32[1,4]{1,0:T(1,128)S(1)}, s32[1,4]{1,0:T(1,128)}, u32[]{:S(2)}) copy-start(s32[1,4]{1,0:T(1,128)} %param.12) | copy-start | bytes 52
  7.2 43.4 %copy-start.4 = (bf16[512,512]{1,0:T(8,128)(2,1)S(1)}, bf16[512,512]{1,0:T(8,128)(2,1)}, u32[]{:S(2)}) copy-start(bf16[512,512]{1,0:T(8,128)(2,1)} %param.17) | copy-start | bytes 1572868
  26.5 25.1 %copy-start.18 = (s32[512,8]{0,1:T(8,128)S(1)}, s32[512,8]{0,1:T(8,128)}, u32[]{:S(2)}) copy-start(s32[512,8]{0,1:T(8,128)} %param.13) | copy-start | bytes 49156
  41.8 43.1 %copy-start.19 = (s32[512]{0:T(512)S(1)}, s32[512]{0:T(512)}, u32[]{:S(2)}) copy-start(s32[512]{0:T(512)} %param.11) | copy-start | bytes 6148
  41.8 25.3 %all-to-all-start.2 = ((bf16[64,4,2,512]{3,2,1,0:T(2,128)(2,1)}), bf16[64,4,2,512]{3,2,1,0:T(2,128)(2,1)S(1)}, u32[]{:S(2)}, u32[]{:S(2)}) async-start(bf16[64,4,2,512]{3,2,1,0:T(2,128)(2,1)} %reshape.215), calls=%async_computation.2 | async-start | bytes 1048576 | tf_op jit(solution)/shard_map/all_to_all | solution.py:80
  68.3 13.5 %all-to-all-start.3 = ((bf16[64,4,2,512]{3,2,0,1:T(2,128)(2,1)}), bf16[64,4,2,512]{3,2,0,1:T(2,128)(2,1)S(1)}, u32[]{:S(2)}, u32[]{:S(2)}) async-start(bf16[64,4,2,512]{3,2,0,1:T(2,128)(2,1)} %copy.146), calls=%async_computation.3 | async-start | bytes 1048576 | tf_op jit(solution)/shard_map/all_to_all | solution.py:79
  71.7 269.6 %all-reduce.9.cloned.1.call-start = ((), (), s32[]{:S(2)}) async-start(), calls=%async_computation.6 | async-start | bytes 11534336 | tf_op jit(solution)/shard_map/psum | solution.py:120
  91.6 1.4 copy-start.7
  98.3 4.9 %copy-start.8 = (bf16[64,4,8,128]{3,2,1,0:T(8,128)(2,1)S(1)}, bf16[64,4,8,128]{3,2,1,0:T(8,128)(2,1)}, u32[]{:S(2)}) copy-start(bf16[64,4,8,128]{3,2,1,0:T(8,128)(2,1)} %get-tuple-element.49) | copy-start | bytes 1572868
  103.1 2.6 copy-start.2
  117.1 5.1 %copy-start.10 = (bf16[512,512]{0,1:T(8,128)(2,1)S(1)}, bf16[512,512]{0,1:T(8,128)(2,1)}, u32[]{:S(2)}) copy-start(bf16[512,512]{0,1:T(8,128)(2,1)} %copy.176) | copy-start | bytes 1572868
  117.1 6.3 %copy-start.11 = (bf16[512,512]{0,1:T(8,128)(2,1)S(1)}, bf16[512,512]{0,1:T(8,128)(2,1)}, u32[]{:S(2)}) copy-start(bf16[512,512]{0,1:T(8,128)(2,1)} %copy.177) | copy-start | bytes 1572868
  122.1 2.9 copy-start.3
  122.2 2.9 copy-start.13
  139.6 1.6 copy-start.9
  139.6 3.9 copy-start.5
  145.0 196.3 %copy-start.20 = (s32[512]{0:T(512)S(1)}, s32[512]{0:T(512)}, u32[]{:S(2)}) copy-start(s32[512]{0:T(512)} %param.11) | copy-start | bytes 6148
  145.0 326.2 %all-reduce.11.cloned.1.call-start = ((), (), s32[]{:S(2)}) async-start(), calls=%async_computation.7 | async-start | bytes 11534336 | tf_op jit(solution)/shard_map/psum | solution.py:119
  341.3 35.2 %copy-start.6 = (bf16[512,512]{1,0:T(8,128)(2,1)S(1)}, bf16[512,512]{1,0:T(8,128)(2,1)}, u32[]{:S(2)}) copy-start(bf16[512,512]{1,0:T(8,128)(2,1)} %get-tuple-element.48) | copy-start | bytes 1572868
  345.9 24.0 %all-to-all-start.4 = ((bf16[64,4,2,512]{3,2,1,0:T(2,128)(2,1)}), bf16[64,4,2,512]{3,2,1,0:T(2,128)(2,1)}, u32[]{:S(2)}, u32[]{:S(2)}) async-start(bf16[64,4,2,512]{3,2,1,0:T(2,128)(2,1)} %reshape.212), calls=%async_computation.4 | async-start | bytes 1048576 | tf_op jit(solution)/shard_map/all_to_all | solution.py:91
  372.1 20.0 %all-to-all-start.5 = ((bf16[64,4,2,512]{3,2,0,1:T(2,128)(2,1)}), bf16[64,4,2,512]{3,2,0,1:T(2,128)(2,1)}, u32[]{:S(2)}, u32[]{:S(2)}) async-start(bf16[64,4,2,512]{3,2,0,1:T(2,128)(2,1)} %copy.164), calls=%async_computation.5 | async-start | bytes 1048576 | tf_op jit(solution)/shard_map/all_to_all | solution.py:90
  471.3 4.9 %copy-start.14 = (f32[512,512]{1,0:T(8,128)S(1)}, f32[512,512]{1,0:T(8,128)}, u32[]{:S(2)}) copy-start(f32[512,512]{1,0:T(8,128)} %get-tuple-element.45) | copy-start | bytes 3145732
  471.3 6.0 %copy-start.15 = (f32[256,512]{1,0:T(8,128)S(1)}, f32[256,512]{1,0:T(8,128)}, u32[]{:S(2)}) copy-start(f32[256,512]{1,0:T(8,128)} %get-tuple-element.43) | copy-start | bytes 1572868
  (4 other events, 3.7 us)
Sparse Core Ops, SparseCore 0:
  145.2 196.0 all-reduce.8
  344.0 127.2 all-reduce.10
